TPU v7x, 32 devices: a whole 2x2x4 slice. The times are simulated.
32 devices in a mesh: pole: 4 (over z), row: 4 (over y, x), col: 2 (over core).
Axes of the slice: x: 2, y: 2, z: 4, core: 2. Of those that a mesh axis runs over, the one named last changes fastest.
Arguments:
- green_blocks: bfloat16 [16, 2, 192, 1536], P('pole', 'col', None, 'row'), parts along dimension 0, may hold values from -0.15625 to 0.15625
- lower_panel: bfloat16 [1536, 32, 128], P(('row', 'col'), 'pole'), parts along dimension 1, may hold values from -1.5 to 1.5
- pattern: int32 [12, 8], replicated, may hold values 0 or 1
- pivot_inverse: float32 [8, 512, 128], P(('row', 'col'), 'pole'), parts along dimension 1, may hold values from -6 to 6
Outputs:
- green_panel: bfloat16 [6144, 8, 128], P('pole', ('row', 'col')), parts along dimension 0
- green_diag: float32 [8, 512, 128], P(('row', 'col'), 'pole'), parts along dimension 1
There are 4 independent parts, one for each index of `pole`. A program takes and returns all parts, laid end to end along the dimension named above; an argument that names none is the same for every part. Nothing has to cross between parts.
All inputs are finite; a program needn't handle non-finite values.
Results may differ from a plain program's by a relative error of at most 0.01.
Values may be sent and summed in bfloat16 or wider, within the bound.
A program may use at most 128 MiB of HBM per device.

v0:
```python
import jax
import jax.numpy as jnp
from jax import lax
from jax.sharding import PartitionSpec as P


def local(green_blocks, lower_panel, pattern, pivot_inverse):
    row_count = lax.axis_size("row")
    col_count = lax.axis_size("col")
    row_share, supernodes, width = lower_panel.shape
    block_count = pattern.shape[0]
    position = lax.axis_index("row") * col_count + lax.axis_index("col")
    row_ids = position * row_share + jnp.arange(row_share, dtype=jnp.int32)
    onehot = (
        row_ids[:, None] // width == jnp.arange(block_count, dtype=jnp.int32)[None, :]
    ).astype(jnp.float32)
    own_mask = jnp.dot(onehot, pattern.astype(jnp.float32), precision=lax.Precision.HIGHEST)
    masked = lower_panel * own_mask[:, :, None].astype(jnp.bfloat16)
    local_green = green_blocks.reshape(-1, green_blocks.shape[3])
    piece = lax.all_gather(masked, "col", axis=0, tiled=True)
    partial_value = jnp.dot(
        local_green, piece.reshape(piece.shape[0], -1), preferred_element_type=jnp.float32
    )
    shaped = partial_value.astype(jnp.bfloat16).reshape(partial_value.shape[0], supernodes, width)
    received = lax.all_to_all(shaped, ("row", "col"), split_axis=1, concat_axis=0, tiled=True)
    kept = received.shape[1]
    received = received.reshape(row_count, col_count, row_count, row_share, kept, width)
    resolved = (
        jnp.sum(received.astype(jnp.float32), axis=0)
        .transpose(1, 0, 2, 3, 4)
        .reshape(-1, kept, width)
    )
    column_panel = lax.all_to_all(masked, ("row", "col"), split_axis=1, concat_axis=0, tiled=True)
    own_columns = lax.dynamic_slice_in_dim(pattern, position * kept, kept, 1)
    column_mask = jnp.repeat(own_columns, width, axis=0).astype(jnp.float32)
    green_panel = (-(resolved * column_mask[:, :, None])).astype(jnp.bfloat16)
    green_diag = pivot_inverse + jnp.einsum(
        "rkb,rkc->kbc", column_panel.astype(jnp.float32), resolved, precision=lax.Precision.HIGHEST
    )
    return (green_panel, green_diag)


def solution(mesh):
    placed = (
        P("pole", "col", None, "row"),
        P(("row", "col"), "pole", None),
        P(),
        P(("row", "col"), "pole", None),
    )
    return jax.shard_map(
        local,
        mesh=mesh,
        in_specs=placed,
        out_specs=(P("pole", ("row", "col"), None), P(("row", "col"), "pole", None)),
        check_vma=False,
    )
```

profile of v0, /device:TPU:0, one launch (start us, length us, event | category | flops | bytes accessed | tf_op | source)
XLA Modules:
  0.0 47.8 jit_solution(6955600791728680446)
XLA Ops:
  0.6 0.0 copy-start
  0.7 0.9 %convolution_convert_fusion.1 = bf16[192,8]{0,1:T(8,128)(2,1)S(1)} fusion(s32[192]{0:T(256)S(1)} %and_select_fusion, s32[12,8]{0,1:T(8,128)} %param.6), kind=kOutput, calls=%fused_computation.4 | convolution fusion | flops 225120 | bytes 4224 | tf_op jit(solution)/shard_map/dot_general | solution.py:17
  1.6 0.2 copy.16
  1.8 1.3 %broadcast_multiply_fusion = bf16[192,8,128]{2,1,0:T(8,128)(2,1)S(1)} fusion(bf16[192,8,128]{2,1,0:T(8,128)(2,1)} %param.5, bf16[192,8]{1,0:T(8,128)(2,1)S(1)} %copy.16), kind=kLoop, calls=%fused_computation.8 | loop fusion | flops 196608 | bytes 789504 | tf_op jit(solution)/shard_map/mul | solution.py:18
  3.1 2.5 %all_gather.3 = bf16[384,8,128]{2,1,0:T(8,128)(2,1)S(1)} all-gather(bf16[192,8,128]{2,1,0:T(8,128)(2,1)S(1)} %broadcast_multiply_fusion), channel_id=1, replica_groups=mesh['pole'=4,'row'=4,'col'=2] {'col'}, dimensions={0}, use_global_device_ids=true | all-gather | bytes 1179648 | tf_op jit(solution)/shard_map/all_gather | solution.py:20
  5.6 0.6 %copy.17 = bf16[384,8,128]{0,2,1:T(8,128)(2,1)S(1)} copy(bf16[384,8,128]{2,1,0:T(8,128)(2,1)S(1)} %all_gather.3) | data formatting | bytes 1572864 | tf_op jit(solution)/shard_map/all_gather | solution.py:20
  6.2 0.0 copy-done
  6.2 1.0 %convolution_convert_fusion = bf16[1024,768]{1,0:T(8,128)(2,1)S(1)} fusion(bf16[384,1024]{0,1:T(8,128)(2,1)S(1)} %bitcast.44, bf16[768,384]{1,0:T(8,128)(2,1)S(1)} %bitcast.38), kind=kOutput, calls=%fused_computation | convolution fusion | flops 604766208 | bytes 2949120 | tf_op jit(solution)/shard_map/dot_general | solution.py:21
  7.2 1.6 %copy.18 = bf16[768,8,128]{2,0,1:T(8,128)(2,1)} copy(bf16[768,8,128]{0,2,1:T(8,128)(2,1)S(1)} %bitcast.42) | data formatting | bytes 3145728 | tf_op jit(solution)/shard_map/reshape | solution.py:24
  8.8 5.1 %all-to-all-start = ((bf16[768,8,128]{2,0,1:T(8,128)(2,1)}), bf16[768,8,128]{2,0,1:T(8,128)(2,1)S(1)}, u32[]{:S(2)}, u32[]{:S(2)}) async-start(bf16[768,8,128]{2,0,1:T(8,128)(2,1)} %copy.18), calls=%async_computation | async-start | bytes 3145728 | tf_op jit(solution)/shard_map/all_to_all | solution.py:25
  13.8 0.8 %copy.20 = bf16[192,8,128]{2,0,1:T(8,128)(2,1)} copy(bf16[192,8,128]{2,1,0:T(8,128)(2,1)S(1)} %broadcast_multiply_fusion) | data formatting | bytes 786432 | tf_op jit(solution)/shard_map/mul | solution.py:18
  14.7 0.7 %convert_bitcast_fusion = f32[12]{0:T(128)S(1)} fusion(s32[12,8]{0,1:T(8,128)} %param.6, s32[]{:T(128)S(6)} %select_n.14), kind=kLoop, calls=%fused_computation.17 | loop fusion | flops 12 | bytes 100 | tf_op jit(solution)/shard_map/convert_element_type | solution.py:35
  15.3 0.1 broadcast_bitcast_fusion
  15.4 19.4 %all-to-all-done = bf16[768,8,128]{2,0,1:T(8,128)(2,1)S(1)} async-done(((bf16[768,8,128]{2,0,1:T(8,128)(2,1)}), bf16[768,8,128]{2,0,1:T(8,128)(2,1)S(1)}, u32[]{:S(2)}, u32[]{:S(2)}) %all-to-all-start) | async-done | bytes 1572896 | tf_op jit(solution)/shard_map/all_to_all | solution.py:25
  34.8 3.5 %all-to-all-start.1 = ((bf16[192,8,128]{2,0,1:T(8,128)(2,1)}), bf16[192,8,128]{2,0,1:T(8,128)(2,1)S(1)}, u32[]{:S(2)}, u32[]{:S(2)}) async-start(bf16[192,8,128]{2,0,1:T(8,128)(2,1)} %copy.20), calls=%async_computation.1 | async-start | bytes 786432 | tf_op jit(solution)/shard_map/all_to_all | solution.py:33
  38.3 1.9 %bitcast_convert_fusion = f32[768,8,1,128]{3,0,1,2:T(8,128)} fusion(bf16[768,8,128]{2,0,1:T(8,128)(2,1)S(1)} %all-to-all-done), kind=kLoop, calls=%fused_computation.1 | loop fusion | flops 786432 | bytes 4718592 | tf_op jit(solution)/shard_map/convert_element_type | solution.py:29
  40.1 2.1 %reduce_sum.11 = f32[2,4,192,128]{3,2,1,0:T(8,128)S(1)} reduce(f32[4,2,4,192,128]{4,3,2,1,0:T(8,128)} %bitcast.39, f32[]{:T(128)} %constant.31.clone.1), dimensions={0}, to_apply=%region_0.1 | reduce | flops 589824 | bytes 3932164 | tf_op jit(solution)/shard_map/reduce_sum | solution.py:29
  42.3 0.0 copy-start.1
  42.3 0.1 copy.19
  42.4 1.0 %fusion.2 = bf16[1536,1,128]{2,0,1:T(8,128)(2,1)} fusion(f32[4,2,192,1,128]{4,2,1,0,3:T(8,128)S(1)} %copy.19, f32[1536]{0:T(1024)S(1)} %broadcast_bitcast_fusion), kind=kLoop, calls=%fused_computation.7 | loop fusion | flops 589824 | bytes 1185792 | tf_op jit(solution)/shard_map/convert_element_type | solution.py:36
  43.4 3.1 %all-to-all-done.1 = bf16[192,8,128]{2,0,1:T(8,128)(2,1)S(1)} async-done(((bf16[192,8,128]{2,0,1:T(8,128)(2,1)}), bf16[192,8,128]{2,0,1:T(8,128)(2,1)S(1)}, u32[]{:S(2)}, u32[]{:S(2)}) %all-to-all-start.1) | async-done | bytes 393248 | tf_op jit(solution)/shard_map/all_to_all | solution.py:33
  46.5 0.0 copy-done.1
  46.5 1.2 %fusion = f32[1,128,128]{2,1,0:T(8,128)} fusion(f32[1,128,128]{2,1,0:T(8,128)S(1)} %copy-done.1, bf16[1536,128]{1,0:T(8,128)(2,1)S(1)} %bitcast.43, f32[1536,128]{1,0:T(8,128)S(1)} %bitcast.40), kind=kOutput, calls=%fused_computation.3 | convolution fusion | flops 302006272 | bytes 1310720 | tf_op jit(solution)/shard_map/rkb,rkc->kbc/dot_general | solution.py:37
  (1 shorter events, 0.0 us)
Async XLA Ops:
  0.6 5.5 %copy-start = (bf16[4,1,192,384]{3,2,1,0:T(8,128)(2,1)S(1)}, bf16[4,1,192,384]{3,2,1,0:T(8,128)(2,1)}, u32[]{:S(2)}) copy-start(bf16[4,1,192,384]{3,2,1,0:T(8,128)(2,1)} %param.4) | copy-start | bytes 1769476
  8.8 26.1 %all-to-all-start = ((bf16[768,8,128]{2,0,1:T(8,128)(2,1)}), bf16[768,8,128]{2,0,1:T(8,128)(2,1)S(1)}, u32[]{:S(2)}, u32[]{:S(2)}) async-start(bf16[768,8,128]{2,0,1:T(8,128)(2,1)} %copy.18), calls=%async_computation | async-start | bytes 3145728 | tf_op jit(solution)/shard_map/all_to_all | solution.py:25
  34.8 11.7 %all-to-all-start.1 = ((bf16[192,8,128]{2,0,1:T(8,128)(2,1)}), bf16[192,8,128]{2,0,1:T(8,128)(2,1)S(1)}, u32[]{:S(2)}, u32[]{:S(2)}) async-start(bf16[192,8,128]{2,0,1:T(8,128)(2,1)} %copy.20), calls=%async_computation.1 | async-start | bytes 786432 | tf_op jit(solution)/shard_map/all_to_all | solution.py:33
  42.3 4.2 %copy-start.1 = (f32[1,128,128]{2,1,0:T(8,128)S(1)}, f32[1,128,128]{2,1,0:T(8,128)}, u32[]{:S(2)}) copy-start(f32[1,128,128]{2,1,0:T(8,128)} %param.7) | copy-start | bytes 196612
where the time goes:
time: 48.2 us; the launch traced here: 47.8 us
  waiting for transfers between devices  22.6 us (47%)
  starting transfers between devices  8.53 us (18%)
  other arithmetic  6.99 us (15%)
  local copies, waits for them, and re-layouts  3.3 us (7%)
  matrix products  3.18 us (7%)
  blocking collectives  2.49 us (5%)
  between operations  0.71 us (1%)
    all_to_all x1, waiting for transfers between devices, local(): lax.all_to_all(shaped, ('row', 'col'), split_axis=1, concat_axis=0, tiled...  19.4 us
    all_to_all x1, starting transfers between devices, local(): lax.all_to_all(shaped, ('row', 'col'), split_axis=1, concat_axis=0, tiled...  5.08 us
    all_to_all x1, starting transfers between devices, local(): lax.all_to_all(masked, ('row', 'col'), split_axis=1, concat_axis=0, tiled...  3.45 us
    all_to_all x1, waiting for transfers between devices, local(): lax.all_to_all(masked, ('row', 'col'), split_axis=1, concat_axis=0, tiled...  3.15 us
    all_gather x1, blocking collectives, local(): piece = lax.all_gather(masked, 'col', axis=0, tiled=True)  2.49 us
    reduce_sum x1, other arithmetic, local(): jnp.sum(received.astype(jnp.float32), axis=0).transpose(1, 0, 2, 3, 4)  2.14 us
    convert_element_type x1, other arithmetic, local(): received.astype(jnp.float32)  1.86 us
    reshape x1, local copies, waits for them, and re-layouts, local(): partial_value.astype(jnp.bfloat16)  1.57 us
  transfers between devices with their start and end apart: 2, of which 2 were waited for; matrix products, arithmetic and copies ran while one was open for 14% of the time, Pallas kernels for 0%

commit v1 on v0

v1 whole, which is shorter than its diff:
```python
import functools

import jax
import jax.numpy as jnp
from jax import lax
from jax.experimental import pallas as pl
from jax.experimental.pallas import tpu as pltpu
from jax.sharding import PartitionSpec as P

MESH = pl.DeviceIdType.MESH
PAIR = 2


def kernel(
    rows, cols, pattern_ref, green_ref, panel_ref, pivot_ref, out_ref, diag_ref,
    slab, column, to_far, from_far, to_x, to_y, to_own, from_own, from_x, from_y,
    slab_send, slab_recv, column_send, column_recv, far_send, far_recv,
    x_send, x_recv, y_send, y_recv, own_send, own_recv,
):
    r, c = lax.axis_index("row"), lax.axis_index("col")
    me = r * cols + c
    share, width = panel_ref.shape[1:]
    half = rows // 2 * share
    row_x, row_y, row_far = r + 1 - 2 * (r % 2), (r + 2) % 4, 3 - r
    halves = (slice(0, half), slice(half, 2 * half))

    def remote(src, dst, send, recv, row, col):
        return pltpu.make_async_remote_copy(
            src_ref=src, dst_ref=dst, send_sem=send, recv_sem=recv,
            device_id={"row": row, "col": col}, device_id_type=MESH,
        )

    barrier = pltpu.get_barrier_semaphore()
    for step in range(1, cols):
        pl.semaphore_signal(barrier, 1, device_id={"row": r, "col": (c + step) % cols}, device_id_type=MESH)
    for row in (row_x, row_y, row_far):
        for k in range(cols):
            pl.semaphore_signal(barrier, 1, device_id={"row": row, "col": k}, device_id_type=MESH)
    slab[c] = panel_ref[...]
    pl.semaphore_wait(barrier, rows * cols - 1)

    started = []

    def start(copy):
        copy.start()
        started.append(copy)

    for step in range(1, cols):
        k = (c + step) % cols
        start(remote(panel_ref, slab.at[c], slab_send.at[k], slab_recv.at[c], r, k))

    def send_column(d, row):
        for k in range(cols):
            start(remote(
                panel_ref.at[row * cols + k], column.at[me],
                column_send.at[d, k], column_recv.at[d, c], row, k,
            ))

    send_column(0, row_x)
    send_column(1, row_y)

    for step in range(1, cols):
        k = (c + step) % cols
        remote(panel_ref, slab.at[k], slab_send.at[k], slab_recv.at[k], r, k).wait_recv()

    chunk = cols * share // width

    def right(row, k):
        parts = []
        for p in range(PAIR):
            supernode = row * cols + k + p
            whole = jnp.concatenate([slab[s, supernode] for s in range(cols)], axis=0)
            blocks = []
            for q in range(chunk):
                flag = pattern_ref[r * chunk + q, supernode].astype(jnp.float32)
                blocks.append((whole[q * width:(q + 1) * width].astype(jnp.float32) * flag).astype(jnp.bfloat16))
            parts.append(jnp.concatenate(blocks, axis=0))
        return jnp.concatenate(parts, axis=1)

    def left(h):
        return green_ref[h * rows // 2:(h + 1) * rows // 2].reshape(half, green_ref.shape[2])

    def product(h, rhs):
        return jnp.dot(left(h), rhs, preferred_element_type=jnp.float32).astype(jnp.bfloat16)

    def over_pairs(body):
        if cols == PAIR:
            body(0)
        else:
            lax.fori_loop(0, cols // PAIR, lambda i, z: (body(i * PAIR), z)[1], 0)

    def far_body(k):
        rhs = right(row_far, k)
        for h in range(2):
            value = product(h, rhs)
            for p in range(PAIR):
                to_far[h, k + p] = value[:, p * width:(p + 1) * width]

    def near_body(row, buffer):
        def body(k):
            rhs = right(row, k)
            for h in range(2):
                value = product(h, rhs)
                for p in range(PAIR):
                    buffer[k + p, halves[h]] = value[:, p * width:(p + 1) * width]
        return body

    over_pairs(far_body)
    start(remote(to_far.at[0], from_far.at[0], far_send.at[0], far_recv.at[0], row_x, c))
    start(remote(to_far.at[1], from_far.at[1], far_send.at[1], far_recv.at[1], row_y, c))

    def send_half(buffer, target, send, recv, h, row):
        for k in range(cols):
            start(remote(
                buffer.at[k, pl.ds(h * half, half)], target.at[c, pl.ds(h * half, half)],
                send.at[h, k], recv.at[h, c], row, k,
            ))

    over_pairs(near_body(row_x, to_x))
    send_half(to_x, from_x, x_send, x_recv, 0, row_x)
    over_pairs(near_body(row_y, to_y))
    send_half(to_y, from_y, y_send, y_recv, 1, row_y)
    send_column(2, row_far)
    over_pairs(near_body(r, to_own))
    for step in range(1, cols):
        k = (c + step) % cols
        start(remote(to_own.at[k], from_own.at[c], own_send.at[k], own_recv.at[c], r, k))
    from_own[c] = to_own[c]

    def add_half(buffer, h):
        for k in range(cols):
            total = buffer[k, halves[h]].astype(jnp.float32) + from_far[h, k].astype(jnp.float32)
            buffer[k, halves[h]] = total.astype(jnp.bfloat16)

    remote(to_far.at[0], from_far.at[0], far_send.at[0], far_recv.at[0], row_x, c).wait_recv()
    add_half(to_y, 0)
    send_half(to_y, from_y, y_send, y_recv, 0, row_y)
    remote(to_far.at[1], from_far.at[1], far_send.at[1], far_recv.at[1], row_y, c).wait_recv()
    add_half(to_x, 1)
    send_half(to_x, from_x, x_send, x_recv, 1, row_x)

    for s in range(cols):
        column[r * cols + s] = slab[s, me]
    for d, row in enumerate((row_x, row_y, row_far)):
        for k in range(cols):
            place = column.at[row * cols + k]
            remote(place, place, column_send.at[d, k], column_recv.at[d, k], row, k).wait_recv()
    for step in range(1, cols):
        k = (c + step) % cols
        remote(to_own.at[k], from_own.at[k], own_send.at[k], own_recv.at[k], r, k).wait_recv()

    def wait_half(target, send, recv, h, row):
        for k in range(cols):
            place = target.at[k, pl.ds(h * half, half)]
            remote(place, place, send.at[h, k], recv.at[h, k], row, k).wait_recv()

    def finish(j):
        span = slice(j * share, (j + 1) * share)
        value = jnp.concatenate(
            [
                from_own[s, span].astype(jnp.float32)
                + from_x[s, span].astype(jnp.float32)
                + from_y[s, span].astype(jnp.float32)
                for s in range(cols)
            ],
            axis=0,
        )
        panel = jnp.concatenate([column[j * cols + s] for s in range(cols)], axis=0)
        blocks = []
        for q in range(chunk):
            flag = pattern_ref[j * chunk + q, me].astype(jnp.float32)
            part = slice(q * width, (q + 1) * width)
            begin = j * chunk * width + q * width
            out_ref[begin:begin + width] = (-(value[part] * flag)).astype(jnp.bfloat16)
            blocks.append((panel[part].astype(jnp.float32) * flag).astype(jnp.bfloat16))
        masked = jnp.concatenate(blocks, axis=0)
        high = value.astype(jnp.bfloat16)
        low = (value - high.astype(jnp.float32)).astype(jnp.bfloat16)
        both = lax.dot_general(
            masked, jnp.concatenate([high, low], axis=1), (((0,), (0,)), ((), ())),
            preferred_element_type=jnp.float32,
        )
        return both[:, :width] + both[:, width:]

    total = pivot_ref[...]
    for h in range(2):
        wait_half(from_x, x_send, x_recv, h, row_x)
        wait_half(from_y, y_send, y_recv, h, row_y)
        for j in range(h * rows // 2, (h + 1) * rows // 2):
            total = total + finish(j)
    diag_ref[...] = total
    for copy in started:
        copy.wait_send()


def local(green_blocks, lower_panel, pattern, pivot_inverse):
    rows, cols = lax.axis_size("row"), lax.axis_size("col")
    share, supernodes, width = lower_panel.shape
    tall = rows * share
    vmem = pl.BlockSpec(memory_space=pltpu.VMEM)
    bf16 = lambda *shape: pltpu.VMEM(shape, jnp.bfloat16)
    dma = lambda *shape: pltpu.SemaphoreType.DMA(shape)
    out, diag = pl.pallas_call(
        functools.partial(kernel, rows, cols),
        out_shape=(
            jax.ShapeDtypeStruct((tall * cols, width), jnp.bfloat16),
            jax.ShapeDtypeStruct((width, width), jnp.float32),
        ),
        in_specs=[pl.BlockSpec(memory_space=pltpu.SMEM), vmem, vmem, vmem],
        out_specs=(vmem, vmem),
        scratch_shapes=[
            bf16(cols, supernodes, share, width),
            bf16(rows * cols, share, width),
            bf16(2, cols, tall // 2, width),
            bf16(2, cols, tall // 2, width),
            bf16(cols, tall, width),
            bf16(cols, tall, width),
            bf16(cols, tall, width),
            bf16(cols, tall, width),
            bf16(cols, tall, width),
            bf16(cols, tall, width),
            dma(cols), dma(cols), dma(3, cols), dma(3, cols), dma(2), dma(2),
            dma(2, cols), dma(2, cols), dma(2, cols), dma(2, cols), dma(cols), dma(cols),
        ],
        compiler_params=pltpu.CompilerParams(
            collective_id=0, has_side_effects=True, vmem_limit_bytes=60 * 1024 * 1024,
        ),
    )(
        pattern,
        green_blocks.reshape(rows, share, -1),
        lower_panel.transpose(1, 0, 2),
        pivot_inverse.reshape(width, width),
    )
    return out.reshape(-1, 1, width), diag.reshape(1, width, width)


def solution(mesh):
    placed = (
        P("pole", "col", None, "row"),
        P(("row", "col"), "pole", None),
        P(),
        P(("row", "col"), "pole", None),
    )
    return jax.shard_map(
        local,
        mesh=mesh,
        in_specs=placed,
        out_specs=(P("pole", ("row", "col"), None), P(("row", "col"), "pole", None)),
        check_vma=False,
    )
```

time: 48.2 us -> 31.1 us (0.65)
  the two profiles are of different devices: /device:TPU:0 before, /device:TPU:1 now
where the time goes in v1:
time: 31.1 us; the launch traced here: 30.9 us
  Pallas kernels  24.7 us (79%)
  local copies, waits for them, and re-layouts  5.59 us (18%)
  between operations  0.65 us (2%)
    pallas_call x1, Pallas kernels, local(): pl.pallas_call(functools.partial(kernel, rows, cols), out_shape=(jax.Shap...  24.7 us
    unnamed x6, local copies, waits for them, and re-layouts  5.59 us

profile of v1, /device:TPU:1, one launch (start us, length us, event | category | flops | bytes accessed | tf_op | source)
XLA Modules:
  0.0 30.9 jit_solution(18077430996127117671)
XLA Ops:
  0.6 1.4 %copy.7.pattern_ref = s32[12,8]{1,0:T(8,128)} copy(s32[12,8]{0,1:T(8,128)} %param.6) | data formatting | bytes 768 | tf_op args[2]
  2.0 1.8 %copy.9 = bf16[192,8,128]{2,0,1:T(8,128)(2,1)} copy(bf16[192,8,128]{2,1,0:T(8,128)(2,1)} %param.5) | data formatting | bytes 786432 | tf_op args[1]
  3.8 24.7 %shard_map.59 = (bf16[1536,128]{1,0:T(8,128)(2,1)}, f32[128,128]{1,0:T(8,128)}) custom-call(s32[12,8]{1,0:T(8,128)} %copy.7.pattern_ref, bf16[4,192,384]{2,1,0:T(8,128)(2,1)} %bitcast.8, bf16[8,192,128]{2,1,0:T(8,128)(2,1)} %bitcast.7, f32[128,128]{1,0:T(8,128)} %bitcast.10), custom_call_target="tpu_custom_call" | custom-call | tf_op jit(solution)/shard_map/pallas_call | solution.py:203
  28.5 0.0 copy-start
  28.5 1.8 %copy.12 = bf16[1536,1,128]{2,0,1:T(8,128)(2,1)} copy(bf16[1536,1,128]{2,0,1:T(8,128)(2,1)} %bitcast.9) | data formatting | bytes 786432
  30.3 0.0 copy-done
  30.3 0.6 %copy.13 = f32[1,128,128]{2,1,0:T(8,128)} copy(f32[1,128,128]{2,1,0:T(8,128)S(1)} %bitcast.11) | data formatting | bytes 131072
Async XLA Ops:
  28.5 1.8 %copy-start = (f32[128,128]{1,0:T(8,128)S(1)}, f32[128,128]{1,0:T(8,128)}, u32[]{:S(2)}) copy-start(f32[128,128]{1,0:T(8,128)} %get-tuple-element.5) | copy-start | bytes 196612

commit v2 on v0

v2 whole, which is shorter than its diff:
```python
import functools
import math

import jax
import jax.numpy as jnp
from jax import lax
from jax.experimental import pallas as pl
from jax.experimental.pallas import tpu as pltpu
from jax.sharding import PartitionSpec as P

MESH = pl.DeviceIdType.MESH
PAIR = 2


def exchange(
    rows, cols, pattern_hbm, green_hbm, panel_hbm, pivot_hbm,
    base, last, column, diag_ref, flags,
    pattern_ref, green_ref, panel_ref, wide, pivot_ref, slab, to_far, from_far, to_x, to_y, to_own, from_own, from_x, from_y,
    load, slab_send, slab_recv, column_send, column_recv, far_send, far_recv,
    x_send, x_recv, y_send, y_recv, own_send, own_recv,
):
    r, c = lax.axis_index("row"), lax.axis_index("col")
    me = r * cols + c
    share, supernodes, width = panel_ref.shape
    mid = rows // 2
    half = mid * share
    row_x, row_y, row_far = r + 1 - 2 * (r % 2), (r + 2) % 4, 3 - r

    def remote(src, dst, send, recv, row, col):
        return pltpu.make_async_remote_copy(
            src_ref=src, dst_ref=dst, send_sem=send, recv_sem=recv,
            device_id={"row": row, "col": col}, device_id_type=MESH,
        )

    barrier = pltpu.get_barrier_semaphore()
    for row in (row_far, row_x, row_y):
        for k in range(cols):
            pl.semaphore_signal(barrier, 1, device_id={"row": row, "col": k}, device_id_type=MESH)
    for step in range(1, cols):
        pl.semaphore_signal(barrier, 1, device_id={"row": r, "col": (c + step) % cols}, device_id_type=MESH)
    loads = [
        pltpu.make_async_copy(panel_hbm, panel_ref, load.at[0]),
        pltpu.make_async_copy(green_hbm, green_ref, load.at[1]),
        pltpu.make_async_copy(pivot_hbm, pivot_ref, load.at[2]),
        pltpu.make_async_copy(pattern_hbm, pattern_ref, load.at[3]),
    ]
    for copy in loads:
        copy.start()

    loads[0].wait()
    loads[3].wait()
    wide[...] = panel_ref[...].astype(jnp.float32).reshape(share * supernodes, width)
    piece = math.gcd(share, width)
    for k in range(supernodes):
        value = wide[pl.ds(k, share, stride=supernodes), :]
        parts = []
        for q in range(share // piece):
            flag = pattern_ref[k, (me * share + q * piece) // width].astype(jnp.float32)
            parts.append(value[q * piece:(q + 1) * piece] * flag)
        slab[c, k] = jnp.concatenate(parts, axis=0).astype(jnp.bfloat16)
    pl.semaphore_wait(barrier, rows * cols - 1)

    started = []

    def start(copy):
        copy.start()
        started.append(copy)

    for step in range(1, cols):
        k = (c + step) % cols
        start(remote(slab.at[c], slab.at[c], slab_send.at[k], slab_recv.at[c], r, k))

    def send_column(d, row):
        for k in range(cols):
            start(remote(
                slab.at[c, row * cols + k], column.at[me],
                column_send.at[d, k], column_recv.at[d, c], row, k,
            ))

    send_column(0, row_x)
    send_column(1, row_y)
    loads[1].wait()

    for step in range(1, cols):
        k = (c + step) % cols
        remote(slab.at[k], slab.at[k], slab_send.at[k], slab_recv.at[k], r, k).wait_recv()

    def product(h, row, k):
        rhs = jnp.concatenate(
            [
                jnp.concatenate([slab[s, row * cols + k + p] for s in range(cols)], axis=0)
                for p in range(PAIR)
            ],
            axis=1,
        )
        lhs = green_ref[h * mid:(h + 1) * mid].reshape(half, green_ref.shape[2])
        value = jnp.dot(lhs, rhs, preferred_element_type=jnp.float32).astype(jnp.bfloat16)
        return value.reshape(mid, share, PAIR * width)

    def fill(buffer, h, row, offset):
        def body(k):
            value = product(h, row, k)
            for p in range(PAIR):
                buffer[k + p, offset:offset + mid] = value[:, :, p * width:(p + 1) * width]

        if cols == PAIR:
            body(0)
        else:
            lax.fori_loop(0, cols // PAIR, lambda i, z: (body(i * PAIR), z)[1], 0)

    for h, row in enumerate((row_x, row_y)):
        fill(to_far.at[h], h, row_far, 0)
        start(remote(to_far.at[h], from_far.at[h], far_send.at[h], far_recv.at[h], row, c))

    def send_direct(buffer, target, send, recv, h, row):
        for k in range(cols):
            start(remote(
                buffer.at[k, pl.ds(h * mid, mid)], target.at[c],
                send.at[h, k], recv.at[h, c], row, k,
            ))

    def send_sum(buffer, send, recv, h, row):
        for k in range(cols):
            start(remote(
                buffer.at[k, pl.ds(h * mid, mid)], last.at[pl.ds(h * mid, mid), c],
                send.at[h, k], recv.at[h, c], row, k,
            ))

    fill(to_x, 0, row_x, 0)
    send_direct(to_x, from_x, x_send, x_recv, 0, row_x)
    fill(to_y, 1, row_y, mid)
    send_direct(to_y, from_y, y_send, y_recv, 1, row_y)
    send_column(2, row_far)
    fill(to_y, 0, row_y, 0)
    fill(to_x, 1, row_x, mid)
    for h in range(2):
        fill(to_own, h, r, h * mid)
    for step in range(1, cols):
        k = (c + step) % cols
        start(remote(to_own.at[k], from_own.at[c], own_send.at[k], own_recv.at[c], r, k))
    from_own[c] = to_own[c]

    for h, row, buffer, send, recv, target in (
        (0, row_x, to_y, y_send, y_recv, row_y), (1, row_y, to_x, x_send, x_recv, row_x)
    ):
        remote(to_far.at[h], from_far.at[h], far_send.at[h], far_recv.at[h], row, c).wait_recv()
        for k in range(cols):
            span = slice(h * mid, (h + 1) * mid)
            total = buffer[k, span].astype(jnp.float32) + from_far[h, k].astype(jnp.float32)
            buffer[k, span] = total.astype(jnp.bfloat16)
        send_sum(buffer, send, recv, h, target)

    for s in range(cols):
        column[r * cols + s] = slab[s, me]
    for i in range(flags.shape[0]):
        flags[i] = jnp.broadcast_to(pattern_ref[me, i].astype(jnp.float32), flags.shape[1:])
    for d, row in enumerate((row_x, row_y, row_far)):
        for k in range(cols):
            place = column.at[row * cols + k]
            remote(place, place, column_send.at[d, k], column_recv.at[d, k], row, k).wait_recv()
    for step in range(1, cols):
        k = (c + step) % cols
        remote(to_own.at[k], from_own.at[k], own_send.at[k], own_recv.at[k], r, k).wait_recv()
    loads[2].wait()
    grown = pivot_ref[...]
    for h, source, send, recv, row in ((0, from_x, x_send, x_recv, row_x), (1, from_y, y_send, y_recv, row_y)):
        for k in range(cols):
            remote(source.at[k], source.at[k], send.at[h, k], recv.at[h, k], row, k).wait_recv()
        for j in range(mid):
            panel = []
            value = []
            for s in range(cols):
                value.append(
                    from_own[s, h * mid + j].astype(jnp.float32) + source[s, j].astype(jnp.float32)
                )
                panel.append(column[(h * mid + j) * cols + s])
                base[h * mid + j, s] = value[-1]
            value = jnp.concatenate(value, axis=0)
            high = value.astype(jnp.bfloat16)
            low = (value - high.astype(jnp.float32)).astype(jnp.bfloat16)
            both = lax.dot_general(
                jnp.concatenate(panel, axis=0), jnp.concatenate([high, low], axis=1),
                (((0,), (0,)), ((), ())), preferred_element_type=jnp.float32,
            )
            grown = grown + (both[:, :width] + both[:, width:])
    diag_ref[...] = grown

    for h, send, recv, row in ((0, y_send, y_recv, row_y), (1, x_send, x_recv, row_x)):
        for k in range(cols):
            place = last.at[pl.ds(h * mid, mid), k]
            remote(place, place, send.at[h, k], recv.at[h, k], row, k).wait_recv()
    for copy in started:
        copy.wait_send()


def finish(base, last, column, grown, flags, out_ref, diag_ref):
    rows, cols, share, width = base.shape
    chunk = cols * share // width
    total = grown[...]
    for j in range(rows):
        late = last[j].reshape(cols * share, width)
        value = base[j].reshape(cols * share, width) + late.astype(jnp.float32)
        for q in range(chunk):
            begin = (j * chunk + q) * width
            part = value[q * width:(q + 1) * width] * flags[j * chunk + q, 0:1]
            out_ref[begin:begin + width] = (-part).astype(jnp.bfloat16)
        panel = column[j * cols:(j + 1) * cols].reshape(cols * share, width)
        total = total + lax.dot_general(
            panel, late, (((0,), (0,)), ((), ())), preferred_element_type=jnp.float32
        )
    diag_ref[...] = total


def local(green_blocks, lower_panel, pattern, pivot_inverse):
    rows, cols = lax.axis_size("row"), lax.axis_size("col")
    share, supernodes, width = lower_panel.shape
    blocks = pattern.shape[0]
    mid = rows // 2
    vmem = pl.BlockSpec(memory_space=pltpu.VMEM)
    hbm = pl.BlockSpec(memory_space=pltpu.HBM)
    bf16 = lambda *shape: pltpu.VMEM(shape, jnp.bfloat16)
    dma = lambda *shape: pltpu.SemaphoreType.DMA(shape)
    green = green_blocks.reshape(rows, share, -1)
    buffers = [
        bf16(*green.shape),
        bf16(*lower_panel.shape),
        pltpu.VMEM((share * supernodes, width), jnp.float32),
        pltpu.VMEM((width, width), jnp.float32),
        bf16(cols, supernodes, share, width),
        bf16(2, cols, mid, share, width),
        bf16(2, cols, mid, share, width),
        bf16(cols, rows, share, width),
        bf16(cols, rows, share, width),
        bf16(cols, rows, share, width),
        bf16(cols, rows, share, width),
        bf16(cols, mid, share, width),
        bf16(cols, mid, share, width),
    ]
    held = sum(math.prod(b.shape) * jnp.dtype(b.dtype).itemsize for b in buffers)
    middle = pl.pallas_call(
        functools.partial(exchange, rows, cols),
        out_shape=(
            pltpu.VMEM((rows, cols, share, width), jnp.float32),
            pltpu.VMEM((rows, cols, share, width), jnp.bfloat16),
            pltpu.VMEM((rows * cols, share, width), jnp.bfloat16),
            pltpu.VMEM((width, width), jnp.float32),
            pltpu.VMEM((blocks, 8, width), jnp.float32),
        ),
        in_specs=[hbm] * 4,
        out_specs=(vmem,) * 5,
        scratch_shapes=[pltpu.SMEM(pattern.shape[::-1], pattern.dtype)] + buffers + [
            dma(4), dma(cols), dma(cols), dma(3, cols), dma(3, cols), dma(2), dma(2),
            dma(2, cols), dma(2, cols), dma(2, cols), dma(2, cols), dma(cols), dma(cols),
        ],
        compiler_params=pltpu.CompilerParams(
            collective_id=0, has_side_effects=True, vmem_limit_bytes=held + held // 4 + 4 * 1024 * 1024,
        ),
    )(*(pltpu.with_memory_space_constraint(a, pltpu.HBM) for a in (pattern.T, green, lower_panel, pivot_inverse.reshape(width, width))))
    out, diag = pl.pallas_call(
        finish,
        out_shape=(
            jax.ShapeDtypeStruct((rows * cols * share, width), jnp.bfloat16),
            jax.ShapeDtypeStruct((width, width), jnp.float32),
        ),
        in_specs=[vmem] * 5,
        out_specs=(vmem, vmem),
        compiler_params=pltpu.CompilerParams(vmem_limit_bytes=16 * 1024 * 1024),
    )(*middle)
    return out.reshape(-1, 1, width), diag.reshape(1, width, width)


def solution(mesh):
    placed = (
        P("pole", "col", None, "row"),
        P(("row", "col"), "pole", None),
        P(),
        P(("row", "col"), "pole", None),
    )
    return jax.shard_map(
        local,
        mesh=mesh,
        in_specs=placed,
        out_specs=(P("pole", ("row", "col"), None), P(("row", "col"), "pole", None)),
        check_vma=False,
    )
```

time: 48.2 us -> 24 us (0.50)
  the two profiles are of different devices: /device:TPU:0 before, /device:TPU:1 now
where the time goes in v2:
time: 24 us; the launch traced here: 23.9 us
  Pallas kernels  23.2 us (97%)
  between operations  0.64 us (3%)
    pallas_call x1, Pallas kernels, local(): pl.pallas_call(functools.partial(exchange, rows, cols), out_shape=(pltpu....  22.3 us
    pallas_call x1, Pallas kernels, local(): pl.pallas_call(finish, out_shape=(jax.ShapeDtypeStruct((rows * cols * sha...  0.94 us

profile of v2, /device:TPU:1, one launch (start us, length us, event | category | flops | bytes accessed | tf_op | source)
XLA Modules:
  0.0 23.9 jit_solution(15655871848434458723)
XLA Ops:
  0.6 22.3 %shard_map.59 = (f32[4,2,192,128]{3,2,1,0:T(8,128)S(1)}, bf16[4,2,192,128]{3,2,1,0:T(8,128)(2,1)S(1)}, bf16[8,192,128]{2,1,0:T(8,128)(2,1)S(1)}, f32[128,128]{1,0:T(8,128)S(1)}, f32[12,8,128]{2,1,0:T(8,128)S(1)}) custom-call(s32[8,12]{1,0:T(8,128)} %bitcast.7, bf16[4,192,384]{2,1,0:T(8,128)(2,1)} %bitcast.5, bf16[192,8,128]{2,1,0:T(8,128)(2,1)} %panel_hbm.1, ...), custom_call_target="tpu_custom_call" | custom-call | tf_op jit(solution)/shard_map/pallas_call | solution.py:240
  22.9 0.9 %shard_map.60 = (bf16[1536,128]{1,0:T(8,128)(2,1)}, f32[128,128]{1,0:T(8,128)}) custom-call(f32[4,2,192,128]{3,2,1,0:T(8,128)S(1)} %get-tuple-element.9.base, bf16[4,2,192,128]{3,2,1,0:T(8,128)(2,1)S(1)} %get-tuple-element.10.last, bf16[8,192,128]{2,1,0:T(8,128)(2,1)S(1)} %get-tuple-element.11.column, f32[128,128]{1,0:T(8,128)S(1)} %get-tuple-element.12.grown, ...), custom_call_target="tpu_custom_call" | custom-call | tf_op jit(solution)/shard_map/pallas_call | solution.py:259

commit v3 on v2

--- a/solution.py
+++ b/solution.py
@@ -33,7 +33,7 @@
         )
 
     barrier = pltpu.get_barrier_semaphore()
-    for row in (row_far, row_x, row_y):
+    for row in (row_x, row_y):
         for k in range(cols):
             pl.semaphore_signal(barrier, 1, device_id={"row": row, "col": k}, device_id_type=MESH)
     for step in range(1, cols):
@@ -58,7 +58,7 @@
             flag = pattern_ref[k, (me * share + q * piece) // width].astype(jnp.float32)
             parts.append(value[q * piece:(q + 1) * piece] * flag)
         slab[c, k] = jnp.concatenate(parts, axis=0).astype(jnp.bfloat16)
-    pl.semaphore_wait(barrier, rows * cols - 1)
+    pl.semaphore_wait(barrier, 3 * cols - 1)
 
     started = []
 
@@ -130,7 +130,6 @@
     send_direct(to_x, from_x, x_send, x_recv, 0, row_x)
     fill(to_y, 1, row_y, mid)
     send_direct(to_y, from_y, y_send, y_recv, 1, row_y)
-    send_column(2, row_far)
     fill(to_y, 0, row_y, 0)
     fill(to_x, 1, row_x, mid)
     for h in range(2):
@@ -144,6 +143,8 @@
         (0, row_x, to_y, y_send, y_recv, row_y), (1, row_y, to_x, x_send, x_recv, row_x)
     ):
         remote(to_far.at[h], from_far.at[h], far_send.at[h], far_recv.at[h], row, c).wait_recv()
+        if h == 0:
+            send_column(2, row_far)
         for k in range(cols):
             span = slice(h * mid, (h + 1) * mid)
             total = buffer[k, span].astype(jnp.float32) + from_far[h, k].astype(jnp.float32)

time: 24 us -> 24 us (level)
  no operation moved by 1% of the time
where the time goes in v3:
time: 24 us; the launch traced here: 23.9 us
  Pallas kernels  23.2 us (97%)
  between operations  0.64 us (3%)
    pallas_call x1, Pallas kernels, local(): pl.pallas_call(functools.partial(exchange, rows, cols), out_shape=(pltpu....  22.3 us
    pallas_call x1, Pallas kernels, local(): pl.pallas_call(finish, out_shape=(jax.ShapeDtypeStruct((rows * cols * sha...  0.94 us

profile of v3, /device:TPU:1, one launch (start us, length us, event | category | flops | bytes accessed | tf_op | source)
XLA Modules:
  0.0 23.9 jit_solution(1458620812054633185)
XLA Ops:
  0.6 22.3 %shard_map.59 = (f32[4,2,192,128]{3,2,1,0:T(8,128)S(1)}, bf16[4,2,192,128]{3,2,1,0:T(8,128)(2,1)S(1)}, bf16[8,192,128]{2,1,0:T(8,128)(2,1)S(1)}, f32[128,128]{1,0:T(8,128)S(1)}, f32[12,8,128]{2,1,0:T(8,128)S(1)}) custom-call(s32[8,12]{1,0:T(8,128)} %bitcast.7, bf16[4,192,384]{2,1,0:T(8,128)(2,1)} %bitcast.5, bf16[192,8,128]{2,1,0:T(8,128)(2,1)} %panel_hbm.1, ...), custom_call_target="tpu_custom_call" | custom-call | tf_op jit(solution)/shard_map/pallas_call | solution.py:241
  22.9 0.9 %shard_map.60 = (bf16[1536,128]{1,0:T(8,128)(2,1)}, f32[128,128]{1,0:T(8,128)}) custom-call(f32[4,2,192,128]{3,2,1,0:T(8,128)S(1)} %get-tuple-element.9.base, bf16[4,2,192,128]{3,2,1,0:T(8,128)(2,1)S(1)} %get-tuple-element.10.last, bf16[8,192,128]{2,1,0:T(8,128)(2,1)S(1)} %get-tuple-element.11.column, f32[128,128]{1,0:T(8,128)S(1)} %get-tuple-element.12.grown, ...), custom_call_target="tpu_custom_call" | custom-call | tf_op jit(solution)/shard_map/pallas_call | solution.py:260
